TPU v7x, 256 devices: a whole 4x4x8 slice. The times are simulated.
256 devices in a mesh: tm: 16 (over z, core), mesh: 16 (over y, x).
Axes of the slice: x: 4, y: 4, z: 8, core: 2. Of those that a mesh axis runs over, the one named last changes fastest.
Arguments:
- diag_blocks: float32 [16, 2048, 128], P('tm', 'mesh'), may hold values from -5 to 10, as said below
- coupling: float32 [16, 2048, 128], P('tm', 'mesh'), may hold values from -4 to 1.2, as said below
- arrow_cols: float32 [16, 64, 2048], P('tm', None, 'mesh'), may hold values from -0.005800485 to 0.005800485
- rhs: float32 [16, 2048], P('tm', 'mesh'), may hold values from -3 to 3
- tip_rhs: float32 [64], replicated, may hold values from -6 to 6
- tip_diag: float32 [64], replicated, may hold values from 4 to 6
- config_shift: float32 [4], replicated, may hold values from 0.001 to 0.3
- config_coupling: float32 [4], replicated, may hold values from 0.99 to 1
- pattern: int32 [16, 16], P('tm', 'mesh'), may hold values 0 or 1
Outputs:
- log_diag: float32 [4, 16, 2048], P(None, 'tm', 'mesh')
- forward: float32 [4, 16, 2048], P(None, 'tm', 'mesh')
- tip_log: float32 [4, 64], replicated
- tip_forward: float32 [4, 64], replicated
Inputs may be any that keep to these rules, and one draw needn't show every extreme that they name: Every tile of diag_blocks is symmetric, and for every setting in the stated ranges the block matrix with diagonal tiles A[t,i] + config_shift[c] I and coupling tiles B[c,t,i] is positive definite. Every tile of coupling is symmetric.
All inputs are finite; a program needn't handle non-finite values. No bound on the sum of `pattern` on one device may be relied on, other than what follows from the above.
Results may differ from a plain program's by a relative error of at most 0.0003.
Values sent between devices are 32-bit elements; how exact they have to be, the bound alone decides.
A program may use at most 128 MiB of HBM per device.

v0:
```python
import functools

import jax
import jax.numpy as jnp
from jax import lax
from jax.experimental import pallas as pl
from jax.experimental.pallas import tpu as pltpu
from jax.sharding import PartitionSpec as P

F32 = jnp.float32
GROUP = 4
HROWS = 72
MESH_ID = pl.DeviceIdType.MESH
VM = pltpu.VMEM
NT = (((1,), (1,)), ((), ()))
NN = (((1,), (0,)), ((), ()))


def vspec():
    return pl.BlockSpec(memory_space=pltpu.VMEM)


def sspec():
    return pl.BlockSpec(memory_space=pltpu.SMEM)


def halves(x):
    high = x.astype(jnp.bfloat16)
    return high, (x - high.astype(F32)).astype(jnp.bfloat16)


def product(a, b, dims):
    ah, al = halves(a)
    bh, bl = halves(b)

    def one(x, y):
        return lax.dot_general(x, y, dims, preferred_element_type=F32)

    return one(ah, bh) + (one(ah, bl) + one(al, bh))


def dot_nt(a, b):
    return product(a, b, NT)


def lane_of(x, j):
    return jnp.broadcast_to(x[:, j : j + 1], x.shape)


def row_of(x, k):
    return jnp.broadcast_to(x[k : k + 1, :], x.shape)


def factor(mats, rows, width):
    tiles, wide = rows // 8, width // 8
    sub = lax.broadcasted_iota(jnp.int32, (8, 128), 0)
    lane = lax.broadcasted_iota(jnp.int32, (8, 128), 1)
    is_row = [sub == k for k in range(8)]
    mats = [list(m) for m in mats]
    pivots = [[None] * tiles for _ in mats]
    for base in range(0, rows, width):
        first = base // 8
        inside = (lane >= base) & (lane < base + width)
        state = []
        for mat in mats:
            panel = [mat[first + u] for u in range(wide)]
            cols = [[lane_of(panel[u], base + j) for u in range(wide)] for j in range(width)]
            panel = [
                jnp.where(inside, jnp.where(lane - base - 8 * u == sub, 1.0, 0.0), panel[u])
                for u in range(wide)
            ]
            ahead = None
            if first + wide < tiles:
                ahead = [
                    [lane_of(mat[first + wide + u], base + j) for j in range(width)]
                    for u in range(wide)
                ]
            state.append((panel, cols, list(panel), [jnp.ones((8, 128), F32)] * wide, ahead))
        for k in range(width):
            tile, row = divmod(k, 8)
            mine = is_row[row]
            for panel, cols, done, piv, _ in state:
                pivot = row_of(cols[k][tile], row)
                inv = 1.0 / pivot
                kept = row_of(panel[tile], row)
                done[tile] = jnp.where(mine, kept, done[tile])
                piv[tile] = jnp.where(mine, pivot, piv[tile])
                kept = kept * inv
                own = cols[k]
                for u in range(wide):
                    new = panel[u] - own[u] * kept
                    panel[u] = jnp.where(mine, kept, new) if u == tile else new
                for j in range(k + 1, width):
                    mult = row_of(cols[j][tile], row) * inv
                    for u in range(wide):
                        new = cols[j][u] - own[u] * mult
                        cols[j][u] = jnp.where(mine, mult, new) if u == tile else new
        for (panel, cols, done, piv, ahead), mat, pivs in zip(state, mats, pivots):
            start = first + wide
            if start < tiles:
                spread = [row_of(panel[j // 8], j % 8) for j in range(width)]
                for u in range(wide):
                    terms = [ahead[u][j] * spread[j] for j in range(width)]
                    while len(terms) > 1:
                        terms = [x + y for x, y in zip(terms[::2], terms[1::2])]
                    mat[start + u] = jnp.where(inside, 0.0, mat[start + u]) - terms[0]
                start += wide
            if start < tiles:
                zero = jnp.zeros((8, 128), F32)
                left = jnp.concatenate([jnp.where(inside, mat[q], 0.0) for q in range(start, tiles)], axis=0)
                right = jnp.concatenate([zero] * first + panel + [zero] * (16 - first - wide), axis=0)
                update = product(left, right, NN)
                for q in range(start, tiles):
                    row = 8 * (q - start)
                    mat[q] = jnp.where(inside, 0.0, mat[q]) - update[row : row + 8, :]
            for u in range(wide):
                mat[first + u] = done[u]
                pivs[first + u] = piv[u]
    return mats, pivots


def inverse_factors(mats, width):
    sub = lax.broadcasted_iota(jnp.int32, (8, 128), 0)
    lane = lax.broadcasted_iota(jnp.int32, (8, 128), 1)
    tiled = [[m[8 * i : 8 * i + 8, :] for i in range(16)] for m in mats]
    done, pivots = factor(tiled, 128, width)
    inverses = [
        jnp.concatenate(
            [
                jnp.where(lane <= sub + 8 * i, d[i] * lax.rsqrt(p[i]), 0.0)
                for i in range(16)
            ],
            axis=0,
        )
        for d, p in zip(done, pivots)
    ]
    return inverses, pivots


def eye128():
    sub = lax.broadcasted_iota(jnp.int32, (128, 128), 0)
    lane = lax.broadcasted_iota(jnp.int32, (128, 128), 1)
    return jnp.where(sub == lane, 1.0, 0.0)


def eliminate(mats, stacks, width):
    inverses, _ = inverse_factors(mats, width)
    out = []
    for stack, inv in zip(stacks, inverses):
        half = dot_nt(stack, inv)
        out.append(dot_nt(half, half[: half.shape[0] - HROWS]))
    return out


def gather_kernel(
    pat_ref, a_ref, c_ref, r_ref, y_ref, ao_ref, co_ref, ro_ref, xo_ref, x_ref,
    near_s, near_r, far_s, far_r, pass_s, pass_r, own,
):
    me = lax.axis_index("tm")
    slot = lax.rem(me, GROUP)
    base = me - slot
    core = lax.rem(slot, 2)
    far_slot = lax.rem(slot + 2, GROUP)
    near = {"tm": me + 1 - 2 * core}
    far = {"tm": base + far_slot}
    barrier = pltpu.get_barrier_semaphore()
    for peer in (near, far):
        pl.semaphore_signal(barrier, inc=1, device_id=peer, device_id_type=MESH_ID)
    x_ref[...] = jnp.zeros((8, 128), F32)
    x_ref[0:1, :] = y_ref[...]
    keep = jnp.where(me > 0, pat_ref[0, 0], 0).astype(F32)
    x_ref[1:2, :] = jnp.full((1, 128), 1.0, F32) * keep
    pl.semaphore_wait(barrier, 2)
    outs = (ao_ref, co_ref, ro_ref, xo_ref)
    mine = (a_ref.at[0], c_ref.at[0], r_ref.at[0], x_ref)

    def send(src, dst, ss, rs, target):
        copy = pltpu.make_async_remote_copy(
            src_ref=src, dst_ref=dst, send_sem=ss, recv_sem=rs, device_id=target, device_id_type=MESH_ID
        )
        copy.start()
        return copy

    far_copies = [
        send(mine[i], outs[i].at[slot], far_s.at[i], far_r.at[i], far) for i in range(4)
    ]
    near_copies = [
        send(mine[i], outs[i].at[slot], near_s.at[i], near_r.at[i], near) for i in range(4)
    ]
    local = [pltpu.make_async_copy(mine[i], outs[i].at[slot], own.at[i]) for i in range(4)]
    for copy in local:
        copy.start()
    passed = []
    for i in range(4):
        far_copies[i].wait_recv()
        passed.append(
            send(outs[i].at[far_slot], outs[i].at[far_slot], pass_s.at[i], pass_r.at[i], near)
        )
    for copy in local:
        copy.wait()
    for copy in far_copies:
        copy.wait_send()
    for copy in near_copies + passed:
        copy.wait()


def group_gather(pattern, diag_blocks, coupling, arrow_cols, rhs):
    dma = pltpu.SemaphoreType.DMA
    return pl.pallas_call(
        gather_kernel,
        out_shape=(
            jax.ShapeDtypeStruct((GROUP, 128, 128), F32),
            jax.ShapeDtypeStruct((GROUP, 128, 128), F32),
            jax.ShapeDtypeStruct((GROUP, 64, 128), F32),
            jax.ShapeDtypeStruct((GROUP, 8, 128), F32),
        ),
        in_specs=[sspec()] + [vspec()] * 4,
        out_specs=(vspec(),) * 4,
        scratch_shapes=[VM((8, 128), F32)] + [dma((4,))] * 7,
        compiler_params=pltpu.CompilerParams(collective_id=0, has_side_effects=True),
    )(pattern, diag_blocks, coupling, arrow_cols, rhs)


class Blocks:
    def __init__(self, a_ref, c_ref, r_ref, x_ref, shift_ref, couple_ref):
        slot = lax.rem(lax.axis_index("tm"), GROUP)
        self.refs = (a_ref, c_ref, r_ref, x_ref)
        self.shift, self.couple = shift_ref[slot], couple_ref[slot]

    def diag(self, i):
        return self.refs[0][i] + self.shift * eye128()

    def coup(self, i):
        return self.refs[1][i] * (self.refs[3][i, 1:2, :] * self.couple)

    def right(self, i):
        x = self.refs[3][i]
        sub = lax.broadcasted_iota(jnp.int32, (8, 128), 0)
        return jnp.concatenate([self.refs[2][i], jnp.where(sub == 0, x, 0.0)], axis=0)


def local_kernel(
    a_ref, c_ref, r_ref, x_ref, shift_ref, couple_ref, d_ref, e_ref, u_ref, h_ref, g_ref, st_ref, wt_ref
):
    blocks = Blocks(a_ref, c_ref, r_ref, x_ref, shift_ref, couple_ref)
    diag, coup, right = blocks.diag, blocks.coup, blocks.right
    m0 = jnp.concatenate([coup(1), coup(0), right(0)], axis=0)
    m2 = jnp.concatenate([coup(3), coup(2), right(2)], axis=0)
    ga, gb = eliminate([diag(0), diag(2)], [m0, m2], 8)
    d1 = diag(1) - ga[0:128, 0:128]
    et1 = -ga[128:256, 0:128]
    u1 = ga[128:256, 128:256]
    h1 = right(1) - ga[256:328, 0:128]
    g1 = -ga[256:328, 128:256]
    d_ref[0] = d1
    e_ref[0] = -ga[0:128, 128:256]
    u_ref[0] = u1
    h_ref[0] = h1
    g_ref[0] = g1
    db = diag(3) - gb[0:128, 0:128]
    eb = -gb[0:128, 128:256]
    ub = gb[128:256, 128:256]
    hb = right(3) - gb[256:328, 0:128]
    gvb = -gb[256:328, 128:256]
    n2 = jnp.concatenate([coup(2), et1, h1], axis=0)
    n3 = jnp.concatenate([eb, et1, h1 + gvb], axis=0)
    gc, gd = eliminate([d1, d1 - ub], [n2, n3], 8)
    d_ref[1] = diag(2) - gc[0:128, 0:128]
    e_ref[1] = -gc[0:128, 128:256]
    u_ref[1] = u1 + gc[128:256, 128:256]
    h_ref[1] = right(2) - gc[256:328, 0:128]
    g_ref[1] = g1 - gc[256:328, 128:256]
    d3 = db - gd[0:128, 0:128]
    h3 = hb - gd[256:328, 0:128]
    d_ref[2] = d3
    e_ref[2] = -gd[0:128, 128:256]
    u_ref[2] = u1 + gd[128:256, 128:256]
    h_ref[2] = h3
    g_ref[2] = g1 - gd[256:328, 128:256]
    st_ref[...] = d3
    wt_ref[...] = h3


def local_phase(gathered, config_shift, config_coupling):
    tile = jax.ShapeDtypeStruct((3, 128, 128), F32)
    rows = jax.ShapeDtypeStruct((3, HROWS, 128), F32)
    return pl.pallas_call(
        local_kernel,
        out_shape=(
            tile, tile, tile, rows, rows,
            jax.ShapeDtypeStruct((128, 128), F32),
            jax.ShapeDtypeStruct((HROWS, 128), F32),
        ),
        in_specs=[vspec()] * 4 + [sspec()] * 2,
        out_specs=(vspec(),) * 7,
    )(*gathered, config_shift, config_coupling)


def chain_kernel(
    segs, st_ref, wt_ref, d_ref, e_ref, u_ref, h_ref, g_ref, sin_ref, win_ref, s_out, w_out,
    send, recv,
):
    tm = lax.axis_index("tm")
    seg = tm // GROUP
    barrier = pltpu.get_barrier_semaphore()
    later = {"tm": tm + GROUP}
    earlier = {"tm": tm - GROUP}

    @pl.when(seg > 0)
    def _():
        pl.semaphore_signal(barrier, inc=1, device_id=earlier, device_id_type=MESH_ID)

    @pl.when(seg < segs - 1)
    def _():
        pl.semaphore_signal(barrier, inc=1, device_id=later, device_id_type=MESH_ID)

    pl.semaphore_wait(barrier, (seg > 0).astype(jnp.int32) + (seg < segs - 1).astype(jnp.int32))

    def copies(s_src, w_src):
        return [
            pltpu.make_async_remote_copy(
                src_ref=src, dst_ref=dst, send_sem=send.at[i], recv_sem=recv.at[i],
                device_id=later, device_id_type=MESH_ID,
            )
            for i, (src, dst) in enumerate([(s_src, sin_ref), (w_src, win_ref)])
        ]

    @pl.when(seg == 0)
    def _():
        out = copies(st_ref, wt_ref)
        for copy in out:
            copy.start()
        sin_ref[...] = eye128()
        win_ref[...] = jnp.zeros((HROWS, 128), F32)
        for copy in out:
            copy.wait_send()

    @pl.when(seg > 0)
    def _():
        out = copies(s_out, w_out)
        out[0].wait_recv()

        @pl.when(seg < segs - 1)
        def _():
            (inverse,), _ = inverse_factors([sin_ref[...] - u_ref[2]], 16)
            half = dot_nt(e_ref[2], inverse)
            s_out[...] = d_ref[2] - dot_nt(half, half)
            out[0].start()
            out[1].wait_recv()
            w_out[...] = h_ref[2] - dot_nt(dot_nt(win_ref[...] + g_ref[2], inverse), half)
            out[1].start()
            for copy in out:
                copy.wait_send()

        @pl.when(seg == segs - 1)
        def _():
            out[1].wait_recv()


def chain_phase(state, solved, parts, segs):
    tile = (128, 128)
    rows = (HROWS, 128)
    dma = pltpu.SemaphoreType.DMA
    return pl.pallas_call(
        functools.partial(chain_kernel, segs),
        out_shape=(jax.ShapeDtypeStruct(tile, F32), jax.ShapeDtypeStruct(rows, F32)),
        in_specs=[vspec()] * 7,
        out_specs=(vspec(),) * 2,
        scratch_shapes=[VM(tile, F32), VM(rows, F32), dma((2,)), dma((2,))],
        compiler_params=pltpu.CompilerParams(collective_id=1, has_side_effects=True),
    )(state, solved, *parts)


def finish_kernel(
    chunks, sin_ref, win_ref, a_ref, c_ref, r_ref, x_ref, shift_ref, couple_ref,
    d_ref, e_ref, u_ref, h_ref, g_ref, gram_ref, lf_ref,
):
    blocks = Blocks(a_ref, c_ref, r_ref, x_ref, shift_ref, couple_ref)
    before, w = sin_ref[...], win_ref[...]
    sub = lax.broadcasted_iota(jnp.int32, (8, 128), 0)
    lane = lax.broadcasted_iota(jnp.int32, (8, 128), 1)
    mats = [before] + [before - u_ref[i] for i in range(3)]
    stacks = [jnp.concatenate([blocks.coup(0), w], axis=0)] + [
        jnp.concatenate([e_ref[i], w + g_ref[i]], axis=0) for i in range(3)
    ]
    diags = [blocks.diag(0)] + [d_ref[i] for i in range(3)]
    rights = [blocks.right(0)] + [h_ref[i] for i in range(3)]
    grams = eliminate(mats, stacks, 8)
    schur = [d - g[0:128, 0:128] for d, g in zip(diags, grams)]
    whole = [h - g[128:200, 0:128] for h, g in zip(rights, grams)]
    inverses, pivots = inverse_factors(schur, 8)
    total = None
    for i in range(GROUP):
        x = dot_nt(whole[i], inverses[i])
        gram = dot_nt(x, x)
        total = gram if total is None else total + gram
        logs = jnp.zeros((8, 128), F32)
        for k in range(16):
            logs = logs + jnp.where(lane == sub + 8 * k, jnp.log(pivots[i][k]), 0.0)
        lf_ref[i] = jnp.zeros((8, 128), F32)
        lf_ref[i, 0:1, :] = 0.5 * jnp.sum(logs, axis=0, keepdims=True)
        lf_ref[i, 1:2, :] = x[64:65, :]
    rows = 64 // chunks
    total = jnp.concatenate([total, jnp.zeros((HROWS, 128 - HROWS), F32)], axis=1)
    for m in range(chunks):
        gram_ref[m] = jnp.zeros((8, 128), F32)
        gram_ref[m, 0:rows, :] = total[rows * m : rows * (m + 1), :]


def finish_phase(sin, win, gathered, config_shift, config_coupling, parts, chunks):
    return pl.pallas_call(
        functools.partial(finish_kernel, chunks),
        out_shape=(
            jax.ShapeDtypeStruct((chunks, 8, 128), F32),
            jax.ShapeDtypeStruct((GROUP, 8, 128), F32),
        ),
        in_specs=[vspec()] * 6 + [sspec()] * 2 + [vspec()] * 5,
        out_specs=(vspec(),) * 2,
    )(sin, win, *gathered, config_shift, config_coupling, *parts)


def tail_kernel(
    chunks, times, gram_ref, lf_ref, lf_in, three_in, one_in, two_in, one_out, two_out,
    lf_s, lf_r, one_s, one_r, two_s, two_r, three_s, three_r,
):
    tm, me = lax.axis_index("tm"), lax.axis_index("mesh")
    slot = lax.rem(tm, GROUP)
    group = [tm - slot + lax.rem(slot + d, GROUP) for d in range(1, GROUP)]
    plane = [lax.rem(me + d, chunks) for d in range(1, chunks)]
    column = [lax.rem(tm + d, times) for d in range(1, times)]
    barrier = pltpu.get_barrier_semaphore()
    targets = [{"mesh": m} for m in plane] + [{"tm": t} for t in column]
    for target in targets:
        pl.semaphore_signal(barrier, inc=1, device_id=target, device_id_type=MESH_ID)
    pl.semaphore_wait(barrier, len(targets))

    def send(src, dst, ss, rs, target):
        copy = pltpu.make_async_remote_copy(
            src_ref=src, dst_ref=dst, send_sem=ss, recv_sem=rs, device_id=target, device_id_type=MESH_ID
        )
        copy.start()
        return copy

    one = [
        send(gram_ref.at[m], one_in.at[me], one_s.at[d], one_r.at[d], {"mesh": m})
        for d, m in enumerate(plane)
    ]
    one_in[me] = gram_ref[me]
    for copy in one:
        copy.wait()
    total = one_in[0]
    for m in range(1, chunks):
        total = total + one_in[m]
    one_out[...] = total
    two_in[tm] = total
    two = [
        send(one_out, two_in.at[tm], two_s.at[d], two_r.at[d], {"tm": t})
        for d, t in enumerate(column)
    ]
    lf = [
        send(lf_ref.at[lax.rem(slot + d + 1, GROUP)], lf_in.at[slot], lf_s.at[d], lf_r.at[d], {"tm": t})
        for d, t in enumerate(group)
    ]
    lf_in[slot] = lf_ref[slot]
    for copy in two:
        copy.wait()
    rows = 64 // chunks
    for c in range(GROUP):
        total = two_in[c]
        for t in range(c + GROUP, times, GROUP):
            total = total + two_in[t]
        two_out[rows * c : rows * (c + 1), :] = total[0:rows, :]
    three = [
        send(two_out, three_in.at[me], three_s.at[d], three_r.at[d], {"mesh": m})
        for d, m in enumerate(plane)
    ]
    three_in[me] = two_out[...]
    for copy in lf + three:
        copy.wait()


def tail_phase(gram, lf, chunks, times):
    dma = pltpu.SemaphoreType.DMA
    rows = GROUP * 64 // chunks
    return pl.pallas_call(
        functools.partial(tail_kernel, chunks, times),
        out_shape=(
            jax.ShapeDtypeStruct((GROUP, 8, 128), F32),
            jax.ShapeDtypeStruct((chunks, rows, 128), F32),
        ),
        in_specs=[vspec()] * 2,
        out_specs=(vspec(),) * 2,
        scratch_shapes=[
            VM((chunks, 8, 128), F32),
            VM((times, 8, 128), F32),
            VM((8, 128), F32),
            VM((rows, 128), F32),
            dma((GROUP - 1,)),
            dma((GROUP - 1,)),
            dma((chunks - 1,)),
            dma((chunks - 1,)),
            dma((times - 1,)),
            dma((times - 1,)),
            dma((chunks - 1,)),
            dma((chunks - 1,)),
        ],
        compiler_params=pltpu.CompilerParams(collective_id=2, has_side_effects=True),
    )(gram, lf)


def tip_kernel(chunks, lf_ref, sum_ref, diag_ref, rhs_ref, log_ref, fwd_ref, tlog_ref, tfwd_ref):
    sub = lax.broadcasted_iota(jnp.int32, (8, 128), 0)
    lane = lax.broadcasted_iota(jnp.int32, (8, 128), 1)
    pad = jnp.zeros((1, 64), F32)
    diag = jnp.concatenate([diag_ref[...], pad], axis=1)
    rhs = jnp.concatenate([rhs_ref[...], pad], axis=1)
    rows = 64 // chunks
    start = []
    for i in range(8):
        on = lane == sub + 8 * i
        column = jnp.sum(jnp.where(on, rhs, 0.0), axis=1, keepdims=True)
        start.append(jnp.where(on, diag, 0.0) + jnp.where(lane == 64, column, 0.0))
    mats = []
    for c in range(GROUP):
        log_ref[c] = lf_ref[c, 0:1, :]
        fwd_ref[c] = lf_ref[c, 1:2, :]
        whole = jnp.concatenate(
            [sum_ref[m, rows * c : rows * (c + 1), :] for m in range(chunks)], axis=0
        )
        mats.append([start[i] - whole[8 * i : 8 * i + 8, :] for i in range(8)])
    done, pivots = factor(mats, 64, 8)
    for c in range(GROUP):
        logs = jnp.zeros((8, 128), F32)
        solved = jnp.zeros((8, 128), F32)
        for i in range(8):
            on = lane == sub + 8 * i
            logs = logs + jnp.where(on, jnp.log(pivots[c][i]), 0.0)
            solved = solved + jnp.where(on, lane_of(done[c][i], 64) * lax.rsqrt(pivots[c][i]), 0.0)
        tlog_ref[c : c + 1, :] = 0.5 * jnp.sum(logs, axis=0, keepdims=True)[:, 0:64]
        tfwd_ref[c : c + 1, :] = jnp.sum(solved, axis=0, keepdims=True)[:, 0:64]


def tip_phase(lf, summed, tip_diag, tip_rhs, chunks):
    wide = jax.ShapeDtypeStruct((GROUP, 1, 128), F32)
    narrow = jax.ShapeDtypeStruct((GROUP, 64), F32)
    return pl.pallas_call(
        functools.partial(tip_kernel, chunks),
        out_shape=(wide, wide, narrow, narrow),
        in_specs=[vspec()] * 4,
        out_specs=(vspec(),) * 4,
    )(lf, summed, tip_diag[None], tip_rhs[None])


def shards(
    diag_blocks, coupling, arrow_cols, rhs, tip_rhs, tip_diag, config_shift, config_coupling, pattern
):
    times, chunks = lax.axis_size("tm"), lax.axis_size("mesh")
    gathered = group_gather(pattern, diag_blocks, coupling, arrow_cols, rhs)
    *parts, state, solved = local_phase(gathered, config_shift, config_coupling)
    sin, win = chain_phase(state, solved, parts, times // GROUP)
    gram, lf = finish_phase(sin, win, gathered, config_shift, config_coupling, parts, chunks)
    lf, summed = tail_phase(gram, lf, chunks, times)
    return tip_phase(lf, summed, tip_diag, tip_rhs, chunks)


def solution(mesh):
    in_specs = (
        P("tm", "mesh", None),
        P("tm", "mesh", None),
        P("tm", None, "mesh"),
        P("tm", "mesh"),
        P(),
        P(),
        P(),
        P(),
        P("tm", "mesh"),
    )
    out_specs = (P(None, "tm", "mesh"), P(None, "tm", "mesh"), P(), P())
    return jax.shard_map(shards, mesh=mesh, in_specs=in_specs, out_specs=out_specs, check_vma=False)
```

profile of v0, /device:TPU:1, one launch (start us, length us, event | category | flops | bytes accessed | tf_op | source)
XLA Modules:
  0.0 87.1 jit_solution(15645233847515632665)
XLA Ops:
  1.3 11.3 %shard_map.120 = (f32[4,128,128]{2,1,0:T(8,128)}, f32[4,128,128]{2,1,0:T(8,128)}, f32[4,64,128]{2,1,0:T(8,128)}, f32[4,8,128]{2,1,0:T(8,128)}) custom-call(s32[1,1]{1,0:T(1,128)S(6)} %copy.13.pat_ref, f32[1,128,128]{2,1,0:T(8,128)} %a_ref.1, f32[1,128,128]{2,1,0:T(8,128)} %c_ref.1, f32[1,64,128]{2,1,0:T(8,128)} %r_ref.1, f32[1,128]{1,0:T(1,128)} %y_ref.1), custom_call_target="tpu_custom_call" | custom-call | tf_op jit(solution)/shard_map/pallas_call | solution.py:209
  12.6 11.0 %shard_map.121 = (f32[3,128,128]{2,1,0:T(8,128)}, f32[3,128,128]{2,1,0:T(8,128)}, f32[3,128,128]{2,1,0:T(8,128)}, f32[3,72,128]{2,1,0:T(8,128)}, f32[3,72,128]{2...) custom-call(f32[4,128,128]{2,1,0:T(8,128)} %get-tuple-element.21.a_ref, f32[4,128,128]{2,1,0:T(8,128)} %get-tuple-element.22.c_ref, ...), custom_call_target="tpu_custom_call" | custom-call | tf_op jit(solution)/shard_map/pallas_call | solution.py:287
  23.6 6.8 %shard_map.122 = (f32[128,128]{1,0:T(8,128)}, f32[72,128]{1,0:T(8,128)}) custom-call(f32[128,128]{1,0:T(8,128)} %get-tuple-element.25.st_ref, f32[72,128]{1,0:T(8,128)} %get-tuple-element.26.wt_ref, f32[3,128,128]{2,1,0:T(8,128)} %get-tuple-element.27.d_ref, f32[3,128,128]{2,1,0:T(8,128)} %get-tuple-element.28.e_ref, ...), custom_call_target="tpu_custom_call" | custom-call | tf_op jit(solution)/shard_map/pallas_call | solution.py:364
  30.5 13.3 %shard_map.123 = (f32[16,8,128]{2,1,0:T(8,128)}, f32[4,8,128]{2,1,0:T(8,128)}) custom-call(f32[128,128]{1,0:T(8,128)} %get-tuple-element.32.sin_ref, f32[72,128]{1,0:T(8,128)} %get-tuple-element.33.win_ref, f32[4,128,128]{2,1,0:T(8,128)} %get-tuple-element.21.a_ref, f32[4,128,128]{2,1,0:T(8,128)} %get-tuple-element.22.c_ref, ...), custom_call_target="tpu_custom_call" | custom-call | tf_op jit(solution)/shard_map/pallas_call | solution.py:411
  43.8 39.4 %shard_map.124 = (f32[4,8,128]{2,1,0:T(8,128)}, f32[16,16,128]{2,1,0:T(8,128)}) custom-call(f32[16,8,128]{2,1,0:T(8,128)} %get-tuple-element.34.gram_ref, f32[4,8,128]{2,1,0:T(8,128)} %get-tuple-element.35.lf_ref), custom_call_target="tpu_custom_call" | custom-call | tf_op jit(solution)/shard_map/pallas_call | solution.py:485
  83.2 3.9 %shard_map.125 = (f32[4,1,128]{2,1,0:T(1,128)}, f32[4,1,128]{2,1,0:T(1,128)}, f32[4,64]{1,0:T(4,128)}, f32[4,64]{1,0:T(4,128)}) custom-call(f32[4,8,128]{2,1,0:T(8,128)} %get-tuple-element.36.lf_ref, f32[16,16,128]{2,1,0:T(8,128)} %get-tuple-element.37.sum_ref, f32[1,64]{1,0:T(1,128)} %bitcast.2, f32[1,64]{1,0:T(1,128)} %bitcast.3), custom_call_target="tpu_custom_call" | custom-call | tf_op jit(solution)/shard_map/pallas_call | solution.py:546
where the time goes:
time: 87.4 us; the launch traced here: 87.1 us
  Pallas kernels  85.8 us (98%)
  between operations  1.3 us (1%)
    pallas_call x1, Pallas kernels, tail_phase(): pl.pallas_call(functools.partial(tail_kernel, chunks, times), out_shape=(...  39.4 us
    pallas_call x1, Pallas kernels, finish_phase(): pl.pallas_call(functools.partial(finish_kernel, chunks), out_shape=(jax.S...  13.3 us
    pallas_call x1, Pallas kernels, group_gather(): pl.pallas_call(gather_kernel, out_shape=(jax.ShapeDtypeStruct((GROUP, 128...  11.3 us
    pallas_call x1, Pallas kernels, local_phase(): pl.pallas_call(local_kernel, out_shape=(tile, tile, tile, rows, rows, jax...  11 us
    pallas_call x1, Pallas kernels, chain_phase(): pl.pallas_call(functools.partial(chain_kernel, segs), out_shape=(jax.Shap...  6.85 us
    pallas_call x1, Pallas kernels, tip_phase(): pl.pallas_call(functools.partial(tip_kernel, chunks), out_shape=(wide, wi...  3.88 us

commit v1 on v0

--- a/solution.py
+++ b/solution.py
@@ -239,10 +239,7 @@
         return jnp.concatenate([self.refs[2][i], jnp.where(sub == 0, x, 0.0)], axis=0)
 
 
-def local_kernel(
-    a_ref, c_ref, r_ref, x_ref, shift_ref, couple_ref, d_ref, e_ref, u_ref, h_ref, g_ref, st_ref, wt_ref
-):
-    blocks = Blocks(a_ref, c_ref, r_ref, x_ref, shift_ref, couple_ref)
+def local_blocks(blocks, d_ref, e_ref, u_ref, h_ref, g_ref):
     diag, coup, right = blocks.diag, blocks.coup, blocks.right
     m0 = jnp.concatenate([coup(1), coup(0), right(0)], axis=0)
     m2 = jnp.concatenate([coup(3), coup(2), right(2)], axis=0)
@@ -265,56 +262,89 @@
     n2 = jnp.concatenate([coup(2), et1, h1], axis=0)
     n3 = jnp.concatenate([eb, et1, h1 + gvb], axis=0)
     gc, gd = eliminate([d1, d1 - ub], [n2, n3], 8)
+    d_ref[2] = db - gd[0:128, 0:128]
+    e_ref[2] = -gd[0:128, 128:256]
+    u_ref[2] = u1 + gd[128:256, 128:256]
+    h_ref[2] = hb - gd[256:328, 0:128]
+    g_ref[2] = g1 - gd[256:328, 128:256]
     d_ref[1] = diag(2) - gc[0:128, 0:128]
     e_ref[1] = -gc[0:128, 128:256]
     u_ref[1] = u1 + gc[128:256, 128:256]
     h_ref[1] = right(2) - gc[256:328, 0:128]
     g_ref[1] = g1 - gc[256:328, 128:256]
-    d3 = db - gd[0:128, 0:128]
-    h3 = hb - gd[256:328, 0:128]
-    d_ref[2] = d3
-    e_ref[2] = -gd[0:128, 128:256]
-    u_ref[2] = u1 + gd[128:256, 128:256]
-    h_ref[2] = h3
-    g_ref[2] = g1 - gd[256:328, 128:256]
-    st_ref[...] = d3
-    wt_ref[...] = h3
-
-
-def local_phase(gathered, config_shift, config_coupling):
-    tile = jax.ShapeDtypeStruct((3, 128, 128), F32)
-    rows = jax.ShapeDtypeStruct((3, HROWS, 128), F32)
-    return pl.pallas_call(
-        local_kernel,
-        out_shape=(
-            tile, tile, tile, rows, rows,
-            jax.ShapeDtypeStruct((128, 128), F32),
-            jax.ShapeDtypeStruct((HROWS, 128), F32),
-        ),
-        in_specs=[vspec()] * 4 + [sspec()] * 2,
-        out_specs=(vspec(),) * 7,
-    )(*gathered, config_shift, config_coupling)
-
-
-def chain_kernel(
-    segs, st_ref, wt_ref, d_ref, e_ref, u_ref, h_ref, g_ref, sin_ref, win_ref, s_out, w_out,
-    send, recv,
+
+
+def start_copy(src, dst, ss, rs, target):
+    copy = pltpu.make_async_remote_copy(
+        src_ref=src, dst_ref=dst, send_sem=ss, recv_sem=rs, device_id=target, device_id_type=MESH_ID
+    )
+    copy.start()
+    return copy
+
+
+def finish_blocks(chunks, blocks, sin_ref, win_ref, wait_w, d_ref, e_ref, u_ref, h_ref, g_ref, gram_ref, lf_ref):
+    sub = lax.broadcasted_iota(jnp.int32, (8, 128), 0)
+    lane = lax.broadcasted_iota(jnp.int32, (8, 128), 1)
+    before = sin_ref[...]
+    inverses, _ = inverse_factors([before] + [before - u_ref[i] for i in range(3)], 8)
+    wait_w()
+    w = win_ref[...]
+    stacks = [jnp.concatenate([blocks.coup(0), w], axis=0)] + [
+        jnp.concatenate([e_ref[i], w + g_ref[i]], axis=0) for i in range(3)
+    ]
+    diags = [blocks.diag(0)] + [d_ref[i] for i in range(3)]
+    rights = [blocks.right(0)] + [h_ref[i] for i in range(3)]
+    schur, whole = [], []
+    for stack, inv, d, h in zip(stacks, inverses, diags, rights):
+        half = dot_nt(stack, inv)
+        gram = dot_nt(half, half[0:128])
+        schur.append(d - gram[0:128])
+        whole.append(h - gram[128:200])
+    inverses, pivots = inverse_factors(schur, 8)
+    total = None
+    for i in range(GROUP):
+        x = dot_nt(whole[i], inverses[i])
+        gram = dot_nt(x, x)
+        total = gram if total is None else total + gram
+        logs = jnp.zeros((8, 128), F32)
+        for k in range(16):
+            logs = logs + jnp.where(lane == sub + 8 * k, jnp.log(pivots[i][k]), 0.0)
+        lf_ref[i] = jnp.where(
+            sub == 0,
+            0.5 * jnp.sum(logs, axis=0, keepdims=True),
+            jnp.where(sub == 1, x[64:65, :], 0.0),
+        )
+    rows = 64 // chunks
+    total = jnp.concatenate([total, jnp.zeros((HROWS, 128 - HROWS), F32)], axis=1)
+    for m in range(chunks):
+        gram_ref[m] = jnp.concatenate(
+            [total[rows * m : rows * (m + 1), :], jnp.zeros((8 - rows, 128), F32)], axis=0
+        )
+
+
+def main_kernel(
+    chunks, times, a_ref, c_ref, r_ref, x_ref, shift_ref, couple_ref, lf_in, three_in,
+    d_ref, e_ref, u_ref, h_ref, g_ref, sin_ref, win_ref, s_out, w_out, gram_ref, lf_ref,
+    one_in, two_in, one_out, two_out, send, recv,
+    lf_s, lf_r, one_s, one_r, two_s, two_r, three_s, three_r,
 ):
-    tm = lax.axis_index("tm")
+    tm, me = lax.axis_index("tm"), lax.axis_index("mesh")
+    slot = lax.rem(tm, GROUP)
     seg = tm // GROUP
+    segs = times // GROUP
+    group = [tm - slot + lax.rem(slot + d, GROUP) for d in range(1, GROUP)]
+    plane = [lax.rem(me + d, chunks) for d in range(1, chunks)]
+    column = [lax.rem(tm + d, times) for d in range(1, times)]
+    later = {"tm": tm + GROUP}
     barrier = pltpu.get_barrier_semaphore()
-    later = {"tm": tm + GROUP}
-    earlier = {"tm": tm - GROUP}
-
-    @pl.when(seg > 0)
-    def _():
-        pl.semaphore_signal(barrier, inc=1, device_id=earlier, device_id_type=MESH_ID)
-
-    @pl.when(seg < segs - 1)
-    def _():
-        pl.semaphore_signal(barrier, inc=1, device_id=later, device_id_type=MESH_ID)
-
-    pl.semaphore_wait(barrier, (seg > 0).astype(jnp.int32) + (seg < segs - 1).astype(jnp.int32))
+    targets = [{"mesh": m} for m in plane] + [{"tm": t} for t in column]
+    for target in targets:
+        pl.semaphore_signal(barrier, inc=1, device_id=target, device_id_type=MESH_ID)
+
+    blocks = Blocks(a_ref, c_ref, r_ref, x_ref, shift_ref, couple_ref)
+    parts = (d_ref, e_ref, u_ref, h_ref, g_ref)
+    local_blocks(blocks, *parts)
+    pl.semaphore_wait(barrier, len(targets))
 
     def copies(s_src, w_src):
         return [
@@ -327,13 +357,11 @@
 
     @pl.when(seg == 0)
     def _():
-        out = copies(st_ref, wt_ref)
+        out = copies(d_ref.at[2], h_ref.at[2])
         for copy in out:
             copy.start()
         sin_ref[...] = eye128()
         win_ref[...] = jnp.zeros((HROWS, 128), F32)
-        for copy in out:
-            copy.wait_send()
 
     @pl.when(seg > 0)
     def _():
@@ -349,121 +377,37 @@
             out[1].wait_recv()
             w_out[...] = h_ref[2] - dot_nt(dot_nt(win_ref[...] + g_ref[2], inverse), half)
             out[1].start()
-            for copy in out:
-                copy.wait_send()
-
+
+    def wait_w():
         @pl.when(seg == segs - 1)
         def _():
-            out[1].wait_recv()
-
-
-def chain_phase(state, solved, parts, segs):
-    tile = (128, 128)
-    rows = (HROWS, 128)
-    dma = pltpu.SemaphoreType.DMA
-    return pl.pallas_call(
-        functools.partial(chain_kernel, segs),
-        out_shape=(jax.ShapeDtypeStruct(tile, F32), jax.ShapeDtypeStruct(rows, F32)),
-        in_specs=[vspec()] * 7,
-        out_specs=(vspec(),) * 2,
-        scratch_shapes=[VM(tile, F32), VM(rows, F32), dma((2,)), dma((2,))],
-        compiler_params=pltpu.CompilerParams(collective_id=1, has_side_effects=True),
-    )(state, solved, *parts)
-
-
-def finish_kernel(
-    chunks, sin_ref, win_ref, a_ref, c_ref, r_ref, x_ref, shift_ref, couple_ref,
-    d_ref, e_ref, u_ref, h_ref, g_ref, gram_ref, lf_ref,
-):
-    blocks = Blocks(a_ref, c_ref, r_ref, x_ref, shift_ref, couple_ref)
-    before, w = sin_ref[...], win_ref[...]
-    sub = lax.broadcasted_iota(jnp.int32, (8, 128), 0)
-    lane = lax.broadcasted_iota(jnp.int32, (8, 128), 1)
-    mats = [before] + [before - u_ref[i] for i in range(3)]
-    stacks = [jnp.concatenate([blocks.coup(0), w], axis=0)] + [
-        jnp.concatenate([e_ref[i], w + g_ref[i]], axis=0) for i in range(3)
-    ]
-    diags = [blocks.diag(0)] + [d_ref[i] for i in range(3)]
-    rights = [blocks.right(0)] + [h_ref[i] for i in range(3)]
-    grams = eliminate(mats, stacks, 8)
-    schur = [d - g[0:128, 0:128] for d, g in zip(diags, grams)]
-    whole = [h - g[128:200, 0:128] for h, g in zip(rights, grams)]
-    inverses, pivots = inverse_factors(schur, 8)
-    total = None
-    for i in range(GROUP):
-        x = dot_nt(whole[i], inverses[i])
-        gram = dot_nt(x, x)
-        total = gram if total is None else total + gram
-        logs = jnp.zeros((8, 128), F32)
-        for k in range(16):
-            logs = logs + jnp.where(lane == sub + 8 * k, jnp.log(pivots[i][k]), 0.0)
-        lf_ref[i] = jnp.zeros((8, 128), F32)
-        lf_ref[i, 0:1, :] = 0.5 * jnp.sum(logs, axis=0, keepdims=True)
-        lf_ref[i, 1:2, :] = x[64:65, :]
-    rows = 64 // chunks
-    total = jnp.concatenate([total, jnp.zeros((HROWS, 128 - HROWS), F32)], axis=1)
-    for m in range(chunks):
-        gram_ref[m] = jnp.zeros((8, 128), F32)
-        gram_ref[m, 0:rows, :] = total[rows * m : rows * (m + 1), :]
-
-
-def finish_phase(sin, win, gathered, config_shift, config_coupling, parts, chunks):
-    return pl.pallas_call(
-        functools.partial(finish_kernel, chunks),
-        out_shape=(
-            jax.ShapeDtypeStruct((chunks, 8, 128), F32),
-            jax.ShapeDtypeStruct((GROUP, 8, 128), F32),
-        ),
-        in_specs=[vspec()] * 6 + [sspec()] * 2 + [vspec()] * 5,
-        out_specs=(vspec(),) * 2,
-    )(sin, win, *gathered, config_shift, config_coupling, *parts)
-
-
-def tail_kernel(
-    chunks, times, gram_ref, lf_ref, lf_in, three_in, one_in, two_in, one_out, two_out,
-    lf_s, lf_r, one_s, one_r, two_s, two_r, three_s, three_r,
-):
-    tm, me = lax.axis_index("tm"), lax.axis_index("mesh")
-    slot = lax.rem(tm, GROUP)
-    group = [tm - slot + lax.rem(slot + d, GROUP) for d in range(1, GROUP)]
-    plane = [lax.rem(me + d, chunks) for d in range(1, chunks)]
-    column = [lax.rem(tm + d, times) for d in range(1, times)]
-    barrier = pltpu.get_barrier_semaphore()
-    targets = [{"mesh": m} for m in plane] + [{"tm": t} for t in column]
-    for target in targets:
-        pl.semaphore_signal(barrier, inc=1, device_id=target, device_id_type=MESH_ID)
-    pl.semaphore_wait(barrier, len(targets))
-
-    def send(src, dst, ss, rs, target):
-        copy = pltpu.make_async_remote_copy(
-            src_ref=src, dst_ref=dst, send_sem=ss, recv_sem=rs, device_id=target, device_id_type=MESH_ID
-        )
-        copy.start()
-        return copy
+            copies(s_out, w_out)[1].wait_recv()
+
+    finish_blocks(chunks, blocks, sin_ref, win_ref, wait_w, *parts, gram_ref, lf_ref)
 
     one = [
-        send(gram_ref.at[m], one_in.at[me], one_s.at[d], one_r.at[d], {"mesh": m})
+        start_copy(gram_ref.at[m], one_in.at[me], one_s.at[d], one_r.at[d], {"mesh": m})
         for d, m in enumerate(plane)
     ]
     one_in[me] = gram_ref[me]
     for copy in one:
-        copy.wait()
+        copy.wait_recv()
     total = one_in[0]
     for m in range(1, chunks):
         total = total + one_in[m]
     one_out[...] = total
     two_in[tm] = total
     two = [
-        send(one_out, two_in.at[tm], two_s.at[d], two_r.at[d], {"tm": t})
+        start_copy(one_out, two_in.at[tm], two_s.at[d], two_r.at[d], {"tm": t})
         for d, t in enumerate(column)
     ]
     lf = [
-        send(lf_ref.at[lax.rem(slot + d + 1, GROUP)], lf_in.at[slot], lf_s.at[d], lf_r.at[d], {"tm": t})
+        start_copy(lf_ref.at[lax.rem(slot + d + 1, GROUP)], lf_in.at[slot], lf_s.at[d], lf_r.at[d], {"tm": t})
         for d, t in enumerate(group)
     ]
     lf_in[slot] = lf_ref[slot]
     for copy in two:
-        copy.wait()
+        copy.wait_recv()
     rows = 64 // chunks
     for c in range(GROUP):
         total = two_in[c]
@@ -471,41 +415,52 @@
             total = total + two_in[t]
         two_out[rows * c : rows * (c + 1), :] = total[0:rows, :]
     three = [
-        send(two_out, three_in.at[me], three_s.at[d], three_r.at[d], {"mesh": m})
+        start_copy(two_out, three_in.at[me], three_s.at[d], three_r.at[d], {"mesh": m})
         for d, m in enumerate(plane)
     ]
     three_in[me] = two_out[...]
     for copy in lf + three:
-        copy.wait()
-
-
-def tail_phase(gram, lf, chunks, times):
+        copy.wait_recv()
+
+    @pl.when(seg < segs - 1)
+    def _():
+        for copy in copies(s_out, w_out):
+            copy.wait_send()
+
+    for copy in one + two + lf + three:
+        copy.wait_send()
+
+
+def main_phase(gathered, config_shift, config_coupling, chunks, times):
     dma = pltpu.SemaphoreType.DMA
     rows = GROUP * 64 // chunks
+    tile, strip = (128, 128), (HROWS, 128)
     return pl.pallas_call(
-        functools.partial(tail_kernel, chunks, times),
+        functools.partial(main_kernel, chunks, times),
         out_shape=(
             jax.ShapeDtypeStruct((GROUP, 8, 128), F32),
             jax.ShapeDtypeStruct((chunks, rows, 128), F32),
         ),
-        in_specs=[vspec()] * 2,
+        in_specs=[vspec()] * 4 + [sspec()] * 2,
         out_specs=(vspec(),) * 2,
-        scratch_shapes=[
+        scratch_shapes=[VM((3,) + tile, F32)] * 3
+        + [VM((3,) + strip, F32)] * 2
+        + [VM(tile, F32), VM(strip, F32)] * 2
+        + [
+            VM((chunks, 8, 128), F32),
+            VM((GROUP, 8, 128), F32),
             VM((chunks, 8, 128), F32),
             VM((times, 8, 128), F32),
             VM((8, 128), F32),
             VM((rows, 128), F32),
-            dma((GROUP - 1,)),
-            dma((GROUP - 1,)),
-            dma((chunks - 1,)),
-            dma((chunks - 1,)),
-            dma((times - 1,)),
-            dma((times - 1,)),
-            dma((chunks - 1,)),
-            dma((chunks - 1,)),
-        ],
-        compiler_params=pltpu.CompilerParams(collective_id=2, has_side_effects=True),
-    )(gram, lf)
+        ]
+        + [dma((2,))] * 2
+        + [dma((GROUP - 1,))] * 2
+        + [dma((chunks - 1,))] * 2
+        + [dma((times - 1,))] * 2
+        + [dma((chunks - 1,))] * 2,
+        compiler_params=pltpu.CompilerParams(collective_id=1, has_side_effects=True),
+    )(*gathered, config_shift, config_coupling)
 
 
 def tip_kernel(chunks, lf_ref, sum_ref, diag_ref, rhs_ref, log_ref, fwd_ref, tlog_ref, tfwd_ref):
@@ -556,10 +511,7 @@
 ):
     times, chunks = lax.axis_size("tm"), lax.axis_size("mesh")
     gathered = group_gather(pattern, diag_blocks, coupling, arrow_cols, rhs)
-    *parts, state, solved = local_phase(gathered, config_shift, config_coupling)
-    sin, win = chain_phase(state, solved, parts, times // GROUP)
-    gram, lf = finish_phase(sin, win, gathered, config_shift, config_coupling, parts, chunks)
-    lf, summed = tail_phase(gram, lf, chunks, times)
+    lf, summed = main_phase(gathered, config_shift, config_coupling, chunks, times)
     return tip_phase(lf, summed, tip_diag, tip_rhs, chunks)
 
 

time: 87.4 us -> 75 us (0.86)
  Pallas kernels: 85.8 us -> 73.5 us
    pallas_call x4 -> x1, Pallas kernels: 70.6 us -> 58.3 us  [main_phase(): pl.pallas_call(functools.partial(main_kernel, chunks, times), out_shape=(...]
where the time goes in v1:
time: 75 us; the launch traced here: 74.8 us
  Pallas kernels  73.5 us (98%)
  between operations  1.29 us (2%)
    pallas_call x1, Pallas kernels, main_phase(): pl.pallas_call(functools.partial(main_kernel, chunks, times), out_shape=(...  58.3 us
    pallas_call x1, Pallas kernels, group_gather(): pl.pallas_call(gather_kernel, out_shape=(jax.ShapeDtypeStruct((GROUP, 128...  11.3 us
    pallas_call x1, Pallas kernels, tip_phase(): pl.pallas_call(functools.partial(tip_kernel, chunks), out_shape=(wide, wi...  3.88 us

profile of v1, /device:TPU:1, one launch (start us, length us, event | category | flops | bytes accessed | tf_op | source)
XLA Modules:
  0.0 74.8 jit_solution(1638821418631233609)
XLA Ops:
  1.3 11.3 %shard_map.120 = (f32[4,128,128]{2,1,0:T(8,128)}, f32[4,128,128]{2,1,0:T(8,128)}, f32[4,64,128]{2,1,0:T(8,128)}, f32[4,8,128]{2,1,0:T(8,128)}) custom-call(s32[1,1]{1,0:T(1,128)S(6)} %copy.13.pat_ref, f32[1,128,128]{2,1,0:T(8,128)} %a_ref.1, f32[1,128,128]{2,1,0:T(8,128)} %c_ref.1, f32[1,64,128]{2,1,0:T(8,128)} %r_ref.1, f32[1,128]{1,0:T(1,128)} %y_ref.1), custom_call_target="tpu_custom_call" | custom-call | tf_op jit(solution)/shard_map/pallas_call | solution.py:209
  12.6 58.3 %shard_map.121 = (f32[4,8,128]{2,1,0:T(8,128)}, f32[16,16,128]{2,1,0:T(8,128)}) custom-call(f32[4,128,128]{2,1,0:T(8,128)} %get-tuple-element.10.a_ref, f32[4,128,128]{2,1,0:T(8,128)} %get-tuple-element.11.c_ref, f32[4,64,128]{2,1,0:T(8,128)} %get-tuple-element.12.r_ref, f32[4,8,128]{2,1,0:T(8,128)} %get-tuple-element.13.x_ref, f32[4]{0:T(128)} %shift_ref.1, ...), custom_call_target="tpu_custom_call" | custom-call | tf_op jit(solution)/shard_map/pallas_call | solution.py:438
  70.9 3.9 %shard_map.122 = (f32[4,1,128]{2,1,0:T(1,128)}, f32[4,1,128]{2,1,0:T(1,128)}, f32[4,64]{1,0:T(4,128)}, f32[4,64]{1,0:T(4,128)}) custom-call(f32[4,8,128]{2,1,0:T(8,128)} %get-tuple-element.14.lf_ref, f32[16,16,128]{2,1,0:T(8,128)} %get-tuple-element.15.sum_ref, f32[1,64]{1,0:T(1,128)} %bitcast.2, f32[1,64]{1,0:T(1,128)} %bitcast.3), custom_call_target="tpu_custom_call" | custom-call | tf_op jit(solution)/shard_map/pallas_call | solution.py:501

commit v2 on v1

--- a/solution.py
+++ b/solution.py
@@ -239,34 +239,37 @@
         return jnp.concatenate([self.refs[2][i], jnp.where(sub == 0, x, 0.0)], axis=0)
 
 
-def local_blocks(blocks, d_ref, e_ref, u_ref, h_ref, g_ref):
+def local_blocks(blocks, send_state, send_right, d_ref, e_ref, u_ref, h_ref, g_ref):
     diag, coup, right = blocks.diag, blocks.coup, blocks.right
     m0 = jnp.concatenate([coup(1), coup(0), right(0)], axis=0)
     m2 = jnp.concatenate([coup(3), coup(2), right(2)], axis=0)
     ga, gb = eliminate([diag(0), diag(2)], [m0, m2], 8)
     d1 = diag(1) - ga[0:128, 0:128]
+    ub = gb[128:256, 128:256]
+    (inv_c, inv_d), _ = inverse_factors([d1, d1 - ub], 8)
+    eb = -gb[0:128, 128:256]
+    half_e = dot_nt(eb, inv_d)
+    d_ref[2] = diag(3) - gb[0:128, 0:128] - dot_nt(half_e, half_e)
+    send_state()
+    h1 = right(1) - ga[256:328, 0:128]
+    gvb = -gb[256:328, 128:256]
+    half_h = dot_nt(h1 + gvb, inv_d)
+    h_ref[2] = right(3) - gb[256:328, 0:128] - dot_nt(half_h, half_e)
+    send_right()
+    u1 = ga[128:256, 128:256]
     et1 = -ga[128:256, 0:128]
-    u1 = ga[128:256, 128:256]
-    h1 = right(1) - ga[256:328, 0:128]
     g1 = -ga[256:328, 128:256]
+    half_t = dot_nt(et1, inv_d)
+    e_ref[2] = -dot_nt(half_e, half_t)
+    u_ref[2] = u1 + dot_nt(half_t, half_t)
+    g_ref[2] = g1 - dot_nt(half_h, half_t)
     d_ref[0] = d1
     e_ref[0] = -ga[0:128, 128:256]
     u_ref[0] = u1
     h_ref[0] = h1
     g_ref[0] = g1
-    db = diag(3) - gb[0:128, 0:128]
-    eb = -gb[0:128, 128:256]
-    ub = gb[128:256, 128:256]
-    hb = right(3) - gb[256:328, 0:128]
-    gvb = -gb[256:328, 128:256]
-    n2 = jnp.concatenate([coup(2), et1, h1], axis=0)
-    n3 = jnp.concatenate([eb, et1, h1 + gvb], axis=0)
-    gc, gd = eliminate([d1, d1 - ub], [n2, n3], 8)
-    d_ref[2] = db - gd[0:128, 0:128]
-    e_ref[2] = -gd[0:128, 128:256]
-    u_ref[2] = u1 + gd[128:256, 128:256]
-    h_ref[2] = hb - gd[256:328, 0:128]
-    g_ref[2] = g1 - gd[256:328, 128:256]
+    half = dot_nt(jnp.concatenate([coup(2), et1, h1], axis=0), inv_c)
+    gc = dot_nt(half, half[0:256])
     d_ref[1] = diag(2) - gc[0:128, 0:128]
     e_ref[1] = -gc[0:128, 128:256]
     u_ref[1] = u1 + gc[128:256, 128:256]
@@ -325,7 +328,7 @@
 def main_kernel(
     chunks, times, a_ref, c_ref, r_ref, x_ref, shift_ref, couple_ref, lf_in, three_in,
     d_ref, e_ref, u_ref, h_ref, g_ref, sin_ref, win_ref, s_out, w_out, gram_ref, lf_ref,
-    one_in, two_in, one_out, two_out, send, recv,
+    one_in, two_in, acc_in, one_out, two_out, send, recv, acc_s, acc_r,
     lf_s, lf_r, one_s, one_r, two_s, two_r, three_s, three_r,
 ):
     tm, me = lax.axis_index("tm"), lax.axis_index("mesh")
@@ -336,15 +339,24 @@
     plane = [lax.rem(me + d, chunks) for d in range(1, chunks)]
     column = [lax.rem(tm + d, times) for d in range(1, times)]
     later = {"tm": tm + GROUP}
+    earlier = {"tm": tm - GROUP}
     barrier = pltpu.get_barrier_semaphore()
-    targets = [{"mesh": m} for m in plane] + [{"tm": t} for t in column]
+    targets = [{"mesh": m} for m in plane] + [{"tm": t} for t in group]
     for target in targets:
         pl.semaphore_signal(barrier, inc=1, device_id=target, device_id_type=MESH_ID)
 
+    @pl.when(seg > 0)
+    def _():
+        pl.semaphore_signal(barrier, inc=1, device_id=earlier, device_id_type=MESH_ID)
+
+    @pl.when(seg < segs - 1)
+    def _():
+        pl.semaphore_signal(barrier, inc=1, device_id=later, device_id_type=MESH_ID)
+
+    greeted = len(targets) + (seg > 0).astype(jnp.int32) + (seg < segs - 1).astype(jnp.int32)
+
     blocks = Blocks(a_ref, c_ref, r_ref, x_ref, shift_ref, couple_ref)
     parts = (d_ref, e_ref, u_ref, h_ref, g_ref)
-    local_blocks(blocks, *parts)
-    pl.semaphore_wait(barrier, len(targets))
 
     def copies(s_src, w_src):
         return [
@@ -355,13 +367,22 @@
             for i, (src, dst) in enumerate([(s_src, sin_ref), (w_src, win_ref)])
         ]
 
-    @pl.when(seg == 0)
-    def _():
-        out = copies(d_ref.at[2], h_ref.at[2])
-        for copy in out:
-            copy.start()
-        sin_ref[...] = eye128()
-        win_ref[...] = jnp.zeros((HROWS, 128), F32)
+    def send_state():
+        pl.semaphore_wait(barrier, greeted)
+
+        @pl.when(seg == 0)
+        def _():
+            copies(d_ref.at[2], h_ref.at[2])[0].start()
+            sin_ref[...] = eye128()
+            win_ref[...] = jnp.zeros((HROWS, 128), F32)
+            acc_in[...] = jnp.zeros((8, 128), F32)
+
+    def send_right():
+        @pl.when(seg == 0)
+        def _():
+            copies(d_ref.at[2], h_ref.at[2])[1].start()
+
+    local_blocks(blocks, send_state, send_right, *parts)
 
     @pl.when(seg > 0)
     def _():
@@ -395,25 +416,55 @@
     total = one_in[0]
     for m in range(1, chunks):
         total = total + one_in[m]
-    one_out[...] = total
-    two_in[tm] = total
-    two = [
-        start_copy(one_out, two_in.at[tm], two_s.at[d], two_r.at[d], {"tm": t})
-        for d, t in enumerate(column)
-    ]
     lf = [
         start_copy(lf_ref.at[lax.rem(slot + d + 1, GROUP)], lf_in.at[slot], lf_s.at[d], lf_r.at[d], {"tm": t})
         for d, t in enumerate(group)
     ]
     lf_in[slot] = lf_ref[slot]
-    for copy in two:
-        copy.wait_recv()
+
+    def pass_sum():
+        return pltpu.make_async_remote_copy(
+            src_ref=one_out, dst_ref=acc_in, send_sem=acc_s, recv_sem=acc_r,
+            device_id=later, device_id_type=MESH_ID,
+        )
+
+    @pl.when(seg > 0)
+    def _():
+        pass_sum().wait_recv()
+
+    total = total + acc_in[...]
+    one_out[...] = total
+
+    @pl.when(seg < segs - 1)
+    def _():
+        pass_sum().start()
+
+    def spread():
+        return [
+            pltpu.make_async_remote_copy(
+                src_ref=one_out, dst_ref=two_in.at[slot], send_sem=two_s.at[d], recv_sem=two_r.at[slot],
+                device_id={"tm": t}, device_id_type=MESH_ID,
+            )
+            for d, t in enumerate(column)
+        ]
+
+    @pl.when(seg == segs - 1)
+    def _():
+        for copy in spread():
+            copy.start()
+        two_in[slot] = total
+
+    for c in range(GROUP):
+        @pl.when(tm != times - GROUP + c)
+        def _():
+            pltpu.make_async_remote_copy(
+                src_ref=one_out, dst_ref=two_in.at[c], send_sem=two_s.at[0], recv_sem=two_r.at[c],
+                device_id=later, device_id_type=MESH_ID,
+            ).wait_recv()
+
     rows = 64 // chunks
     for c in range(GROUP):
-        total = two_in[c]
-        for t in range(c + GROUP, times, GROUP):
-            total = total + two_in[t]
-        two_out[rows * c : rows * (c + 1), :] = total[0:rows, :]
+        two_out[rows * c : rows * (c + 1), :] = two_in[c, 0:rows, :]
     three = [
         start_copy(two_out, three_in.at[me], three_s.at[d], three_r.at[d], {"mesh": m})
         for d, m in enumerate(plane)
@@ -426,8 +477,14 @@
     def _():
         for copy in copies(s_out, w_out):
             copy.wait_send()
-
-    for copy in one + two + lf + three:
+        pass_sum().wait_send()
+
+    @pl.when(seg == segs - 1)
+    def _():
+        for copy in spread():
+            copy.wait_send()
+
+    for copy in one + lf + three:
         copy.wait_send()
 
 
@@ -450,14 +507,16 @@
             VM((chunks, 8, 128), F32),
             VM((GROUP, 8, 128), F32),
             VM((chunks, 8, 128), F32),
-            VM((times, 8, 128), F32),
+            VM((GROUP, 8, 128), F32),
+            VM((8, 128), F32),
             VM((8, 128), F32),
             VM((rows, 128), F32),
         ]
         + [dma((2,))] * 2
+        + [dma] * 2
         + [dma((GROUP - 1,))] * 2
         + [dma((chunks - 1,))] * 2
-        + [dma((times - 1,))] * 2
+        + [dma((times - 1,)), dma((GROUP,))]
         + [dma((chunks - 1,))] * 2,
         compiler_params=pltpu.CompilerParams(collective_id=1, has_side_effects=True),
     )(*gathered, config_shift, config_coupling)

time: 75 us -> 74.3 us (level)
  no operation moved by 1% of the time
where the time goes in v2:
time: 74.3 us; the launch traced here: 74.2 us
  Pallas kernels  72.9 us (98%)
  between operations  1.29 us (2%)
    pallas_call x1, Pallas kernels, main_phase(): pl.pallas_call(functools.partial(main_kernel, chunks, times), out_shape=(...  57.6 us
    pallas_call x1, Pallas kernels, group_gather(): pl.pallas_call(gather_kernel, out_shape=(jax.ShapeDtypeStruct((GROUP, 128...  11.3 us
    pallas_call x1, Pallas kernels, tip_phase(): pl.pallas_call(functools.partial(tip_kernel, chunks), out_shape=(wide, wi...  3.88 us

profile of v2, /device:TPU:1, one launch (start us, length us, event | category | flops | bytes accessed | tf_op | source)
XLA Modules:
  0.0 74.2 jit_solution(8648293159221247205)
XLA Ops:
  1.3 11.3 %shard_map.120 = (f32[4,128,128]{2,1,0:T(8,128)}, f32[4,128,128]{2,1,0:T(8,128)}, f32[4,64,128]{2,1,0:T(8,128)}, f32[4,8,128]{2,1,0:T(8,128)}) custom-call(s32[1,1]{1,0:T(1,128)S(6)} %copy.13.pat_ref, f32[1,128,128]{2,1,0:T(8,128)} %a_ref.1, f32[1,128,128]{2,1,0:T(8,128)} %c_ref.1, f32[1,64,128]{2,1,0:T(8,128)} %r_ref.1, f32[1,128]{1,0:T(1,128)} %y_ref.1), custom_call_target="tpu_custom_call" | custom-call | tf_op jit(solution)/shard_map/pallas_call | solution.py:209
  12.6 57.6 %shard_map.121 = (f32[4,8,128]{2,1,0:T(8,128)}, f32[16,16,128]{2,1,0:T(8,128)}) custom-call(f32[4,128,128]{2,1,0:T(8,128)} %get-tuple-element.10.a_ref, f32[4,128,128]{2,1,0:T(8,128)} %get-tuple-element.11.c_ref, f32[4,64,128]{2,1,0:T(8,128)} %get-tuple-element.12.r_ref, f32[4,8,128]{2,1,0:T(8,128)} %get-tuple-element.13.x_ref, f32[4]{0:T(128)} %shift_ref.1, ...), custom_call_target="tpu_custom_call" | custom-call | tf_op jit(solution)/shard_map/pallas_call | solution.py:495
  70.3 3.9 %shard_map.122 = (f32[4,1,128]{2,1,0:T(1,128)}, f32[4,1,128]{2,1,0:T(1,128)}, f32[4,64]{1,0:T(4,128)}, f32[4,64]{1,0:T(4,128)}) custom-call(f32[4,8,128]{2,1,0:T(8,128)} %get-tuple-element.14.lf_ref, f32[16,16,128]{2,1,0:T(8,128)} %get-tuple-element.15.sum_ref, f32[1,64]{1,0:T(1,128)} %bitcast.2, f32[1,64]{1,0:T(1,128)} %bitcast.3), custom_call_target="tpu_custom_call" | custom-call | tf_op jit(solution)/shard_map/pallas_call | solution.py:560

commit v3 on v2

--- a/solution.py
+++ b/solution.py
@@ -80,21 +80,18 @@
             tile, row = divmod(k, 8)
             mine = is_row[row]
             for panel, cols, done, piv, _ in state:
-                pivot = row_of(cols[k][tile], row)
-                inv = 1.0 / pivot
-                kept = row_of(panel[tile], row)
-                done[tile] = jnp.where(mine, kept, done[tile])
-                piv[tile] = jnp.where(mine, pivot, piv[tile])
-                kept = kept * inv
-                own = cols[k]
+                inv = row_of(1.0 / cols[k][tile], row)
+                done[tile] = jnp.where(mine, panel[tile], done[tile])
+                piv[tile] = jnp.where(mine, cols[k][tile], piv[tile])
+                kept = row_of(panel[tile], row) * inv
+                own = list(cols[k])
+                own[tile] = jnp.where(mine, own[tile] - 1.0, own[tile])
                 for u in range(wide):
-                    new = panel[u] - own[u] * kept
-                    panel[u] = jnp.where(mine, kept, new) if u == tile else new
+                    panel[u] = panel[u] - own[u] * kept
                 for j in range(k + 1, width):
                     mult = row_of(cols[j][tile], row) * inv
                     for u in range(wide):
-                        new = cols[j][u] - own[u] * mult
-                        cols[j][u] = jnp.where(mine, mult, new) if u == tile else new
+                        cols[j][u] = cols[j][u] - own[u] * mult
         for (panel, cols, done, piv, ahead), mat, pivs in zip(state, mats, pivots):
             start = first + wide
             if start < tiles:
@@ -209,10 +206,10 @@
     return pl.pallas_call(
         gather_kernel,
         out_shape=(
-            jax.ShapeDtypeStruct((GROUP, 128, 128), F32),
-            jax.ShapeDtypeStruct((GROUP, 128, 128), F32),
-            jax.ShapeDtypeStruct((GROUP, 64, 128), F32),
-            jax.ShapeDtypeStruct((GROUP, 8, 128), F32),
+            VM((GROUP, 128, 128), F32),
+            VM((GROUP, 128, 128), F32),
+            VM((GROUP, 64, 128), F32),
+            VM((GROUP, 8, 128), F32),
         ),
         in_specs=[sspec()] + [vspec()] * 4,
         out_specs=(vspec(),) * 4,
@@ -285,7 +282,7 @@
     return copy
 
 
-def finish_blocks(chunks, blocks, sin_ref, win_ref, wait_w, d_ref, e_ref, u_ref, h_ref, g_ref, gram_ref, lf_ref):
+def finish_blocks(blocks, sin_ref, win_ref, wait_w, d_ref, e_ref, u_ref, h_ref, g_ref, sum_ref, lf_ref):
     sub = lax.broadcasted_iota(jnp.int32, (8, 128), 0)
     lane = lax.broadcasted_iota(jnp.int32, (8, 128), 1)
     before = sin_ref[...]
@@ -317,19 +314,41 @@
             0.5 * jnp.sum(logs, axis=0, keepdims=True),
             jnp.where(sub == 1, x[64:65, :], 0.0),
         )
-    rows = 64 // chunks
     total = jnp.concatenate([total, jnp.zeros((HROWS, 128 - HROWS), F32)], axis=1)
-    for m in range(chunks):
-        gram_ref[m] = jnp.concatenate(
-            [total[rows * m : rows * (m + 1), :], jnp.zeros((8 - rows, 128), F32)], axis=0
-        )
+    wide_lane = lax.broadcasted_iota(jnp.int32, (32, 128), 1)
+    sum_ref[0:32, :] = jnp.where(wide_lane < 64, total[0:32], pltpu.roll(total[32:64], 64, 1))
+    sum_ref[32:40, :] = total[64:72]
+
+
+def solve_tip(packed, tip_diag, tip_rhs):
+    sub = lax.broadcasted_iota(jnp.int32, (8, 128), 0)
+    lane = lax.broadcasted_iota(jnp.int32, (8, 128), 1)
+    pad = jnp.zeros((1, 64), F32)
+    diag = jnp.concatenate([tip_diag, pad], axis=1)
+    rhs = jnp.concatenate([tip_rhs, pad], axis=1) - packed[32:33]
+    gram = jnp.concatenate([packed[0:32], pltpu.roll(packed[0:32], 64, 1)], axis=0)
+    mat = []
+    for i in range(8):
+        on = lane == sub + 8 * i
+        column = jnp.sum(jnp.where(on, rhs, 0.0), axis=1, keepdims=True)
+        own = jnp.where(on, diag, 0.0) - gram[8 * i : 8 * i + 8]
+        mat.append(jnp.where(lane < 64, own, jnp.where(lane == 64, column, 0.0)))
+    (done,), (pivots,) = factor([mat], 64, 8)
+    logs = jnp.zeros((8, 128), F32)
+    solved = jnp.zeros((8, 128), F32)
+    for i in range(8):
+        on = lane == sub + 8 * i
+        logs = logs + jnp.where(on, jnp.log(pivots[i]), 0.0)
+        solved = solved + jnp.where(on, lane_of(done[i], 64) * lax.rsqrt(pivots[i]), 0.0)
+    logs = 0.5 * jnp.sum(logs, axis=0, keepdims=True)
+    return jnp.where(sub == 0, logs, jnp.sum(solved, axis=0, keepdims=True))
 
 
 def main_kernel(
-    chunks, times, a_ref, c_ref, r_ref, x_ref, shift_ref, couple_ref, lf_in, three_in,
-    d_ref, e_ref, u_ref, h_ref, g_ref, sin_ref, win_ref, s_out, w_out, gram_ref, lf_ref,
-    one_in, two_in, acc_in, one_out, two_out, send, recv, acc_s, acc_r,
-    lf_s, lf_r, one_s, one_r, two_s, two_r, three_s, three_r,
+    chunks, times, a_ref, c_ref, r_ref, x_ref, shift_ref, couple_ref, tdiag_ref, trhs_ref, lf_in, tip_in,
+    d_ref, e_ref, u_ref, h_ref, g_ref, sin_ref, win_ref, s_out, w_out, sum_ref, lf_ref,
+    plane_in, acc_in, tip_out, send, recv, acc_s, acc_r,
+    lf_s, lf_r, plane_s, plane_r, tip_s, tip_r,
 ):
     tm, me = lax.axis_index("tm"), lax.axis_index("mesh")
     slot = lax.rem(tm, GROUP)
@@ -375,7 +394,7 @@
             copies(d_ref.at[2], h_ref.at[2])[0].start()
             sin_ref[...] = eye128()
             win_ref[...] = jnp.zeros((HROWS, 128), F32)
-            acc_in[...] = jnp.zeros((8, 128), F32)
+            acc_in[...] = jnp.zeros((40, 128), F32)
 
     def send_right():
         @pl.when(seg == 0)
@@ -391,7 +410,7 @@
 
         @pl.when(seg < segs - 1)
         def _():
-            (inverse,), _ = inverse_factors([sin_ref[...] - u_ref[2]], 16)
+            (inverse,), _ = inverse_factors([sin_ref[...] - u_ref[2]], 8)
             half = dot_nt(e_ref[2], inverse)
             s_out[...] = d_ref[2] - dot_nt(half, half)
             out[0].start()
@@ -404,18 +423,8 @@
         def _():
             copies(s_out, w_out)[1].wait_recv()
 
-    finish_blocks(chunks, blocks, sin_ref, win_ref, wait_w, *parts, gram_ref, lf_ref)
-
-    one = [
-        start_copy(gram_ref.at[m], one_in.at[me], one_s.at[d], one_r.at[d], {"mesh": m})
-        for d, m in enumerate(plane)
-    ]
-    one_in[me] = gram_ref[me]
-    for copy in one:
-        copy.wait_recv()
-    total = one_in[0]
-    for m in range(1, chunks):
-        total = total + one_in[m]
+    finish_blocks(blocks, sin_ref, win_ref, wait_w, *parts, sum_ref, lf_ref)
+
     lf = [
         start_copy(lf_ref.at[lax.rem(slot + d + 1, GROUP)], lf_in.at[slot], lf_s.at[d], lf_r.at[d], {"tm": t})
         for d, t in enumerate(group)
@@ -424,7 +433,7 @@
 
     def pass_sum():
         return pltpu.make_async_remote_copy(
-            src_ref=one_out, dst_ref=acc_in, send_sem=acc_s, recv_sem=acc_r,
+            src_ref=sum_ref, dst_ref=acc_in, send_sem=acc_s, recv_sem=acc_r,
             device_id=later, device_id_type=MESH_ID,
         )
 
@@ -432,46 +441,45 @@
     def _():
         pass_sum().wait_recv()
 
-    total = total + acc_in[...]
-    one_out[...] = total
+    total = sum_ref[...] + acc_in[...]
+    sum_ref[...] = total
 
     @pl.when(seg < segs - 1)
     def _():
         pass_sum().start()
 
-    def spread():
-        return [
-            pltpu.make_async_remote_copy(
-                src_ref=one_out, dst_ref=two_in.at[slot], send_sem=two_s.at[d], recv_sem=two_r.at[slot],
-                device_id={"tm": t}, device_id_type=MESH_ID,
-            )
+    @pl.when(seg == segs - 1)
+    def _():
+        share = [
+            start_copy(sum_ref, plane_in.at[me], plane_s.at[d], plane_r.at[d], {"mesh": m})
+            for d, m in enumerate(plane)
+        ]
+        plane_in[me] = total
+        for copy in share:
+            copy.wait_recv()
+        whole = plane_in[0]
+        for m in range(1, chunks):
+            whole = whole + plane_in[m]
+        result = solve_tip(whole, tdiag_ref[...], trhs_ref[...])
+        tip_out[...] = result
+        spread = [
+            start_copy(tip_out, tip_in.at[slot], tip_s.at[d], tip_r.at[slot], {"tm": t})
             for d, t in enumerate(column)
         ]
-
-    @pl.when(seg == segs - 1)
-    def _():
-        for copy in spread():
-            copy.start()
-        two_in[slot] = total
-
+        tip_in[slot] = result
+        for copy in share + spread:
+            copy.wait_send()
+
+    for copy in lf:
+        copy.wait()
     for c in range(GROUP):
+
         @pl.when(tm != times - GROUP + c)
         def _():
             pltpu.make_async_remote_copy(
-                src_ref=one_out, dst_ref=two_in.at[c], send_sem=two_s.at[0], recv_sem=two_r.at[c],
+                src_ref=tip_out, dst_ref=tip_in.at[c], send_sem=tip_s.at[0], recv_sem=tip_r.at[c],
                 device_id=later, device_id_type=MESH_ID,
             ).wait_recv()
-
-    rows = 64 // chunks
-    for c in range(GROUP):
-        two_out[rows * c : rows * (c + 1), :] = two_in[c, 0:rows, :]
-    three = [
-        start_copy(two_out, three_in.at[me], three_s.at[d], three_r.at[d], {"mesh": m})
-        for d, m in enumerate(plane)
-    ]
-    three_in[me] = two_out[...]
-    for copy in lf + three:
-        copy.wait_recv()
 
     @pl.when(seg < segs - 1)
     def _():
@@ -479,90 +487,51 @@
             copy.wait_send()
         pass_sum().wait_send()
 
-    @pl.when(seg == segs - 1)
-    def _():
-        for copy in spread():
-            copy.wait_send()
-
-    for copy in one + lf + three:
-        copy.wait_send()
-
-
-def main_phase(gathered, config_shift, config_coupling, chunks, times):
+
+def main_phase(gathered, config_shift, config_coupling, tip_diag, tip_rhs, chunks, times):
     dma = pltpu.SemaphoreType.DMA
-    rows = GROUP * 64 // chunks
     tile, strip = (128, 128), (HROWS, 128)
     return pl.pallas_call(
         functools.partial(main_kernel, chunks, times),
-        out_shape=(
-            jax.ShapeDtypeStruct((GROUP, 8, 128), F32),
-            jax.ShapeDtypeStruct((chunks, rows, 128), F32),
-        ),
-        in_specs=[vspec()] * 4 + [sspec()] * 2,
+        out_shape=(VM((GROUP, 8, 128), F32), VM((GROUP, 8, 128), F32)),
+        in_specs=[vspec()] * 4 + [sspec()] * 2 + [vspec()] * 2,
         out_specs=(vspec(),) * 2,
         scratch_shapes=[VM((3,) + tile, F32)] * 3
         + [VM((3,) + strip, F32)] * 2
         + [VM(tile, F32), VM(strip, F32)] * 2
         + [
-            VM((chunks, 8, 128), F32),
+            VM((40, 128), F32),
             VM((GROUP, 8, 128), F32),
-            VM((chunks, 8, 128), F32),
-            VM((GROUP, 8, 128), F32),
+            VM((chunks, 40, 128), F32),
+            VM((40, 128), F32),
             VM((8, 128), F32),
-            VM((8, 128), F32),
-            VM((rows, 128), F32),
         ]
         + [dma((2,))] * 2
         + [dma] * 2
         + [dma((GROUP - 1,))] * 2
         + [dma((chunks - 1,))] * 2
-        + [dma((times - 1,)), dma((GROUP,))]
-        + [dma((chunks - 1,))] * 2,
+        + [dma((times - 1,)), dma((GROUP,))],
         compiler_params=pltpu.CompilerParams(collective_id=1, has_side_effects=True),
-    )(*gathered, config_shift, config_coupling)
-
-
-def tip_kernel(chunks, lf_ref, sum_ref, diag_ref, rhs_ref, log_ref, fwd_ref, tlog_ref, tfwd_ref):
-    sub = lax.broadcasted_iota(jnp.int32, (8, 128), 0)
-    lane = lax.broadcasted_iota(jnp.int32, (8, 128), 1)
-    pad = jnp.zeros((1, 64), F32)
-    diag = jnp.concatenate([diag_ref[...], pad], axis=1)
-    rhs = jnp.concatenate([rhs_ref[...], pad], axis=1)
-    rows = 64 // chunks
-    start = []
-    for i in range(8):
-        on = lane == sub + 8 * i
-        column = jnp.sum(jnp.where(on, rhs, 0.0), axis=1, keepdims=True)
-        start.append(jnp.where(on, diag, 0.0) + jnp.where(lane == 64, column, 0.0))
-    mats = []
+    )(*gathered, config_shift, config_coupling, tip_diag[None], tip_rhs[None])
+
+
+def write_kernel(lf_ref, tip_ref, log_ref, fwd_ref, tlog_ref, tfwd_ref):
     for c in range(GROUP):
         log_ref[c] = lf_ref[c, 0:1, :]
         fwd_ref[c] = lf_ref[c, 1:2, :]
-        whole = jnp.concatenate(
-            [sum_ref[m, rows * c : rows * (c + 1), :] for m in range(chunks)], axis=0
-        )
-        mats.append([start[i] - whole[8 * i : 8 * i + 8, :] for i in range(8)])
-    done, pivots = factor(mats, 64, 8)
-    for c in range(GROUP):
-        logs = jnp.zeros((8, 128), F32)
-        solved = jnp.zeros((8, 128), F32)
-        for i in range(8):
-            on = lane == sub + 8 * i
-            logs = logs + jnp.where(on, jnp.log(pivots[c][i]), 0.0)
-            solved = solved + jnp.where(on, lane_of(done[c][i], 64) * lax.rsqrt(pivots[c][i]), 0.0)
-        tlog_ref[c : c + 1, :] = 0.5 * jnp.sum(logs, axis=0, keepdims=True)[:, 0:64]
-        tfwd_ref[c : c + 1, :] = jnp.sum(solved, axis=0, keepdims=True)[:, 0:64]
-
-
-def tip_phase(lf, summed, tip_diag, tip_rhs, chunks):
+        tlog_ref[c : c + 1, :] = tip_ref[c, 0:1, 0:64]
+        tfwd_ref[c : c + 1, :] = tip_ref[c, 1:2, 0:64]
+
+
+def write_phase(lf, tip):
     wide = jax.ShapeDtypeStruct((GROUP, 1, 128), F32)
     narrow = jax.ShapeDtypeStruct((GROUP, 64), F32)
     return pl.pallas_call(
-        functools.partial(tip_kernel, chunks),
+        write_kernel,
         out_shape=(wide, wide, narrow, narrow),
-        in_specs=[vspec()] * 4,
+        in_specs=[vspec()] * 2,
         out_specs=(vspec(),) * 4,
-    )(lf, summed, tip_diag[None], tip_rhs[None])
+    )(lf, tip)
 
 
 def shards(
@@ -570,8 +539,9 @@
 ):
     times, chunks = lax.axis_size("tm"), lax.axis_size("mesh")
     gathered = group_gather(pattern, diag_blocks, coupling, arrow_cols, rhs)
-    lf, summed = main_phase(gathered, config_shift, config_coupling, chunks, times)
-    return tip_phase(lf, summed, tip_diag, tip_rhs, chunks)
+    gathered = [pltpu.with_memory_space_constraint(v, pltpu.VMEM) for v in gathered]
+    results = main_phase(gathered, config_shift, config_coupling, tip_diag, tip_rhs, chunks, times)
+    return write_phase(*[pltpu.with_memory_space_constraint(v, pltpu.VMEM) for v in results])
 
 
 def solution(mesh):

time: 74.3 us -> 68.7 us (0.925)
  Pallas kernels: 72.9 us -> 67.2 us
    pallas_call x2, Pallas kernels: 15.2 us -> 11.1 us  [the longest x1 10.5 us: group_gather(): pl.pallas_call(gather_kernel, out_shape=(VM((GROUP, 128, 128), F32), VM((...]
    pallas_call x1, Pallas kernels: 57.6 us -> 56.1 us  [main_phase(): pl.pallas_call(functools.partial(main_kernel, chunks, times), out_shape=(...]
where the time goes in v3:
time: 68.7 us; the launch traced here: 68.5 us
  Pallas kernels  67.2 us (98%)
  between operations  1.29 us (2%)
    pallas_call x1, Pallas kernels, main_phase(): pl.pallas_call(functools.partial(main_kernel, chunks, times), out_shape=(...  56.1 us
    pallas_call x1, Pallas kernels, group_gather(): pl.pallas_call(gather_kernel, out_shape=(VM((GROUP, 128, 128), F32), VM((...  10.5 us

profile of v3, /device:TPU:1, one launch (start us, length us, event | category | flops | bytes accessed | tf_op | source)
XLA Modules:
  0.0 68.5 jit_solution(7816273341012063688)
XLA Ops:
  1.3 10.5 %shard_map.120 = (f32[4,128,128]{2,1,0:T(8,128)S(1)}, f32[4,128,128]{2,1,0:T(8,128)S(1)}, f32[4,64,128]{2,1,0:T(8,128)S(1)}, f32[4,8,128]{2,1,0:T(8,128)S(1)}) custom-call(s32[1,1]{1,0:T(1,128)S(6)} %copy.13.pat_ref, f32[1,128,128]{2,1,0:T(8,128)} %a_ref.1, f32[1,128,128]{2,1,0:T(8,128)} %c_ref.1, f32[1,64,128]{2,1,0:T(8,128)} %r_ref.1, f32[1,128]{1,0:T(1,128)} %y_ref.1), custom_call_target="tpu_custom_call" | custom-call | tf_op jit(solution)/shard_map/pallas_call | solution.py:206
  11.8 56.1 %shard_map.121 = (f32[4,8,128]{2,1,0:T(8,128)S(1)}, f32[4,8,128]{2,1,0:T(8,128)S(1)}) custom-call(f32[4,128,128]{2,1,0:T(8,128)S(1)} %get-tuple-element.10.a_ref, f32[4,128,128]{2,1,0:T(8,128)S(1)} %get-tuple-element.11.c_ref, f32[4,64,128]{2,1,0:T(8,128)S(1)} %get-tuple-element.12.r_ref, f32[4,8,128]{2,1,0:T(8,128)S(1)} %get-tuple-element.13.x_ref, ...), custom_call_target="tpu_custom_call" | custom-call | tf_op jit(solution)/shard_map/pallas_call | solution.py:494
  67.9 0.6 shard_map.122

commit v4 on v3

--- a/solution.py
+++ b/solution.py
@@ -83,15 +83,16 @@
                 inv = row_of(1.0 / cols[k][tile], row)
                 done[tile] = jnp.where(mine, panel[tile], done[tile])
                 piv[tile] = jnp.where(mine, cols[k][tile], piv[tile])
-                kept = row_of(panel[tile], row) * inv
                 own = list(cols[k])
                 own[tile] = jnp.where(mine, own[tile] - 1.0, own[tile])
+                own = [part * inv for part in own]
+                kept = row_of(panel[tile], row)
                 for u in range(wide):
                     panel[u] = panel[u] - own[u] * kept
                 for j in range(k + 1, width):
-                    mult = row_of(cols[j][tile], row) * inv
+                    kept = row_of(cols[j][tile], row)
                     for u in range(wide):
-                        cols[j][u] = cols[j][u] - own[u] * mult
+                        cols[j][u] = cols[j][u] - own[u] * kept
         for (panel, cols, done, piv, ahead), mat, pivs in zip(state, mats, pivots):
             start = first + wide
             if start < tiles:
@@ -243,7 +244,7 @@
     ga, gb = eliminate([diag(0), diag(2)], [m0, m2], 8)
     d1 = diag(1) - ga[0:128, 0:128]
     ub = gb[128:256, 128:256]
-    (inv_c, inv_d), _ = inverse_factors([d1, d1 - ub], 8)
+    (inv_d,), _ = inverse_factors([d1 - ub], 8)
     eb = -gb[0:128, 128:256]
     half_e = dot_nt(eb, inv_d)
     d_ref[2] = diag(3) - gb[0:128, 0:128] - dot_nt(half_e, half_e)
@@ -265,6 +266,7 @@
     u_ref[0] = u1
     h_ref[0] = h1
     g_ref[0] = g1
+    (inv_c,), _ = inverse_factors([d1], 8)
     half = dot_nt(jnp.concatenate([coup(2), et1, h1], axis=0), inv_c)
     gc = dot_nt(half, half[0:256])
     d_ref[1] = diag(2) - gc[0:128, 0:128]
@@ -308,10 +310,10 @@
         total = gram if total is None else total + gram
         logs = jnp.zeros((8, 128), F32)
         for k in range(16):
-            logs = logs + jnp.where(lane == sub + 8 * k, jnp.log(pivots[i][k]), 0.0)
+            logs = logs + jnp.where(lane == sub + 8 * k, pivots[i][k], 0.0)
         lf_ref[i] = jnp.where(
             sub == 0,
-            0.5 * jnp.sum(logs, axis=0, keepdims=True),
+            0.5 * jnp.log(jnp.sum(logs, axis=0, keepdims=True)),
             jnp.where(sub == 1, x[64:65, :], 0.0),
         )
     total = jnp.concatenate([total, jnp.zeros((HROWS, 128 - HROWS), F32)], axis=1)
@@ -389,9 +391,14 @@
     def send_state():
         pl.semaphore_wait(barrier, greeted)
 
+        def begin(_, carry):
+            copies(d_ref.at[2], h_ref.at[2])[0].start()
+            return carry
+
+        lax.fori_loop(0, (seg == 0).astype(jnp.int32), begin, 0)
+
         @pl.when(seg == 0)
         def _():
-            copies(d_ref.at[2], h_ref.at[2])[0].start()
             sin_ref[...] = eye128()
             win_ref[...] = jnp.zeros((HROWS, 128), F32)
             acc_in[...] = jnp.zeros((40, 128), F32)

time: 68.7 us -> 71 us (1.033)
  Pallas kernels: 67.2 us -> 69.5 us
    pallas_call x1, Pallas kernels: 56.1 us -> 58.4 us  [main_phase(): pl.pallas_call(functools.partial(main_kernel, chunks, times), out_shape=(...]
where the time goes in v4:
time: 71 us; the launch traced here: 70.8 us
  Pallas kernels  69.5 us (98%)
  between operations  1.29 us (2%)
    pallas_call x1, Pallas kernels, main_phase(): pl.pallas_call(functools.partial(main_kernel, chunks, times), out_shape=(...  58.4 us
    pallas_call x1, Pallas kernels, group_gather(): pl.pallas_call(gather_kernel, out_shape=(VM((GROUP, 128, 128), F32), VM((...  10.5 us

profile of v4, /device:TPU:1, one launch (start us, length us, event | category | flops | bytes accessed | tf_op | source)
XLA Modules:
  0.0 70.8 jit_solution(4155123792725446871)
XLA Ops:
  1.3 10.5 %shard_map.120 = (f32[4,128,128]{2,1,0:T(8,128)S(1)}, f32[4,128,128]{2,1,0:T(8,128)S(1)}, f32[4,64,128]{2,1,0:T(8,128)S(1)}, f32[4,8,128]{2,1,0:T(8,128)S(1)}) custom-call(s32[1,1]{1,0:T(1,128)S(6)} %copy.13.pat_ref, f32[1,128,128]{2,1,0:T(8,128)} %a_ref.1, f32[1,128,128]{2,1,0:T(8,128)} %c_ref.1, f32[1,64,128]{2,1,0:T(8,128)} %r_ref.1, f32[1,128]{1,0:T(1,128)} %y_ref.1), custom_call_target="tpu_custom_call" | custom-call | tf_op jit(solution)/shard_map/pallas_call | solution.py:207
  11.8 58.4 %shard_map.121 = (f32[4,8,128]{2,1,0:T(8,128)S(1)}, f32[4,8,128]{2,1,0:T(8,128)S(1)}) custom-call(f32[4,128,128]{2,1,0:T(8,128)S(1)} %get-tuple-element.10.a_ref, f32[4,128,128]{2,1,0:T(8,128)S(1)} %get-tuple-element.11.c_ref, f32[4,64,128]{2,1,0:T(8,128)S(1)} %get-tuple-element.12.r_ref, f32[4,8,128]{2,1,0:T(8,128)S(1)} %get-tuple-element.13.x_ref, ...), custom_call_target="tpu_custom_call" | custom-call | tf_op jit(solution)/shard_map/pallas_call | solution.py:501
  70.2 0.6 shard_map.122

commit v5 on v4

--- a/solution.py
+++ b/solution.py
@@ -244,7 +244,7 @@
     ga, gb = eliminate([diag(0), diag(2)], [m0, m2], 8)
     d1 = diag(1) - ga[0:128, 0:128]
     ub = gb[128:256, 128:256]
-    (inv_d,), _ = inverse_factors([d1 - ub], 8)
+    (inv_c, inv_d), _ = inverse_factors([d1, d1 - ub], 8)
     eb = -gb[0:128, 128:256]
     half_e = dot_nt(eb, inv_d)
     d_ref[2] = diag(3) - gb[0:128, 0:128] - dot_nt(half_e, half_e)
@@ -266,7 +266,6 @@
     u_ref[0] = u1
     h_ref[0] = h1
     g_ref[0] = g1
-    (inv_c,), _ = inverse_factors([d1], 8)
     half = dot_nt(jnp.concatenate([coup(2), et1, h1], axis=0), inv_c)
     gc = dot_nt(half, half[0:256])
     d_ref[1] = diag(2) - gc[0:128, 0:128]
@@ -335,7 +334,7 @@
         column = jnp.sum(jnp.where(on, rhs, 0.0), axis=1, keepdims=True)
         own = jnp.where(on, diag, 0.0) - gram[8 * i : 8 * i + 8]
         mat.append(jnp.where(lane < 64, own, jnp.where(lane == 64, column, 0.0)))
-    (done,), (pivots,) = factor([mat], 64, 8)
+    (done,), (pivots,) = factor([mat], 64, 16)
     logs = jnp.zeros((8, 128), F32)
     solved = jnp.zeros((8, 128), F32)
     for i in range(8):
@@ -417,7 +416,7 @@
 
         @pl.when(seg < segs - 1)
         def _():
-            (inverse,), _ = inverse_factors([sin_ref[...] - u_ref[2]], 8)
+            (inverse,), _ = inverse_factors([sin_ref[...] - u_ref[2]], 16)
             half = dot_nt(e_ref[2], inverse)
             s_out[...] = d_ref[2] - dot_nt(half, half)
             out[0].start()

time: 71 us -> 66.8 us (0.941)
  Pallas kernels: 69.5 us -> 65.4 us
    pallas_call x1, Pallas kernels: 58.4 us -> 54.3 us  [main_phase(): pl.pallas_call(functools.partial(main_kernel, chunks, times), out_shape=(...]
where the time goes in v5:
time: 66.8 us; the launch traced here: 66.7 us
  Pallas kernels  65.4 us (98%)
  between operations  1.29 us (2%)
    pallas_call x1, Pallas kernels, main_phase(): pl.pallas_call(functools.partial(main_kernel, chunks, times), out_shape=(...  54.3 us
    pallas_call x1, Pallas kernels, group_gather(): pl.pallas_call(gather_kernel, out_shape=(VM((GROUP, 128, 128), F32), VM((...  10.5 us

profile of v5, /device:TPU:1, one launch (start us, length us, event | category | flops | bytes accessed | tf_op | source)
XLA Modules:
  0.0 66.7 jit_solution(11291736733774313784)
XLA Ops:
  1.3 10.5 %shard_map.120 = (f32[4,128,128]{2,1,0:T(8,128)S(1)}, f32[4,128,128]{2,1,0:T(8,128)S(1)}, f32[4,64,128]{2,1,0:T(8,128)S(1)}, f32[4,8,128]{2,1,0:T(8,128)S(1)}) custom-call(s32[1,1]{1,0:T(1,128)S(6)} %copy.13.pat_ref, f32[1,128,128]{2,1,0:T(8,128)} %a_ref.1, f32[1,128,128]{2,1,0:T(8,128)} %c_ref.1, f32[1,64,128]{2,1,0:T(8,128)} %r_ref.1, f32[1,128]{1,0:T(1,128)} %y_ref.1), custom_call_target="tpu_custom_call" | custom-call | tf_op jit(solution)/shard_map/pallas_call | solution.py:207
  11.8 54.3 %shard_map.121 = (f32[4,8,128]{2,1,0:T(8,128)S(1)}, f32[4,8,128]{2,1,0:T(8,128)S(1)}) custom-call(f32[4,128,128]{2,1,0:T(8,128)S(1)} %get-tuple-element.10.a_ref, f32[4,128,128]{2,1,0:T(8,128)S(1)} %get-tuple-element.11.c_ref, f32[4,64,128]{2,1,0:T(8,128)S(1)} %get-tuple-element.12.r_ref, f32[4,8,128]{2,1,0:T(8,128)S(1)} %get-tuple-element.13.x_ref, ...), custom_call_target="tpu_custom_call" | custom-call | tf_op jit(solution)/shard_map/pallas_call | solution.py:500
  66.1 0.6 shard_map.122
